TPU v7x, 32 devices: a whole 2x2x4 slice. The times are simulated.
32 devices in a mesh: layer: 16 (over z, x, core), src: 2 (over y).
Axes of the slice: x: 2, y: 2, z: 4, core: 2. Of those that a mesh axis runs over, the one named last changes fastest.
Arguments:
- down_maps: bfloat16 [16, 1664, 1664], P('layer'), may hold values from -1 to 1
- up_maps: bfloat16 [16, 1664, 1664], P('layer'), may hold values from -1 to 1
- local_traces: bfloat16 [128, 1664], P('src'), may hold values from -6 to 6
- src_depth: int32 [128], P('src'), may hold values from 0 to 15
Outputs:
- traces: bfloat16 [16, 128, 1664], P('layer', 'src')
- residual: bfloat16 [16, 128, 1664], P('layer', 'src')
All inputs are finite; a program needn't handle non-finite values.
Results may differ from a plain program's by a relative error of at most 0.035.
Values may be sent and summed in bfloat16 or wider, within the bound.
A program may use at most 64 MiB of HBM per device.

v0:
```python
import jax
import jax.numpy as jnp
from jax import lax
from jax.sharding import PartitionSpec as P


def shifted(shard, axis, by):
    count = lax.axis_size(axis)
    pairs = [(i, i + by) for i in range(count) if 0 <= i + by < count]
    return lax.ppermute(shard, axis, pairs)


def padded_2(cells, sides, width):
    for axis, dim in sides:
        count = lax.axis_size(axis)
        ends = count - 1
        head = lax.slice_in_dim(cells, 0, width, axis=dim)
        tail = lax.slice_in_dim(cells, cells.shape[dim] - width, cells.shape[dim], axis=dim)
        cells = jnp.concatenate(
            [
                lax.ppermute(tail, axis, [(i, (i + 1) % count) for i in range(ends)]),
                cells,
                lax.ppermute(head, axis, [((i + 1) % count, i) for i in range(ends)]),
            ],
            axis=dim,
        )
    return cells


def apply_stack(maps, forcing_block, entering, layer_order):
    results = [None] * maps.shape[0]
    current = entering
    for position in layer_order:
        fresh = forcing_block[position] + jnp.dot(
            current, maps[position], preferred_element_type=jnp.float32
        )
        results[position] = fresh
        current = fresh.astype(jnp.bfloat16)
    return (jnp.stack(results), current)


def advance(maps, forcing, stored, arrived, step_index, lag, block_rows, batch_count, layer_order):
    batch_index = step_index - lag
    active = jnp.logical_and(batch_index >= 0, batch_index < batch_count)
    row_start = jnp.clip(batch_index, 0, batch_count - 1) * block_rows

    def compute_block():
        return apply_stack(maps, forcing, arrived, layer_order)

    def skip_block():
        return (jnp.zeros(forcing.shape, jnp.float32), jnp.zeros(arrived.shape, jnp.bfloat16))

    new_block, leaving = lax.cond(active, compute_block, skip_block)
    previous = stored
    stored = lax.dynamic_update_slice_in_dim(
        stored, jnp.where(active, new_block, previous), row_start, 1
    )
    return (stored, leaving)


def shards(down_maps, up_maps, local_traces, src_depth):
    depth_count = down_maps.shape[0]
    source_rows, trace_width = local_traces.shape
    chain_len = lax.axis_size("layer")
    my_index = lax.axis_index("layer")
    layer_ids = my_index * depth_count + jnp.arange(depth_count, dtype=jnp.int32)
    placed = src_depth[None, :] == layer_ids[:, None]
    forcing = jnp.where(
        placed[:, :, None], local_traces.astype(jnp.float32)[None], jnp.float32(0.0)
    )
    batch_count = source_rows // source_rows
    turn_count = chain_len + batch_count - 1
    downward_order = list(range(depth_count))
    upward_order = downward_order[::-1]
    empty_store = jnp.zeros(forcing.shape, jnp.float32)
    empty_edge = jnp.zeros((source_rows, trace_width), jnp.bfloat16)
    up_lag = chain_len - 1 - my_index

    def joint_turn(step_index, state_tuple):
        down_store, down_edge, up_store, up_edge = state_tuple
        down_store, down_out = advance(
            down_maps,
            forcing,
            down_store,
            down_edge,
            step_index,
            my_index,
            source_rows,
            batch_count,
            downward_order,
        )
        up_store, up_out = advance(
            up_maps,
            forcing,
            up_store,
            up_edge,
            step_index,
            up_lag,
            source_rows,
            batch_count,
            upward_order,
        )
        down_edge = shifted(down_out, "layer", 1)
        up_edge = shifted(up_out, "layer", -1)
        return (down_store, down_edge, up_store, up_edge)

    down_store, _, up_store, _ = lax.fori_loop(
        0, turn_count, joint_turn, (empty_store, empty_edge, empty_store, empty_edge)
    )
    combined = down_store + up_store - forcing
    rounded = combined.astype(jnp.bfloat16)
    padded = padded_2(rounded, (("layer", 0),), 1)
    from_above = jnp.einsum(
        "lsw,lwv->lsv", padded[:-2], down_maps, preferred_element_type=jnp.float32
    )
    from_below = jnp.einsum("lsw,lwv->lsv", padded[2:], up_maps, preferred_element_type=jnp.float32)
    remainder = forcing - combined + from_above + from_below
    return (rounded, remainder.astype(jnp.bfloat16))


def solution(mesh):
    placed = (P("layer", None, None), P("layer", None, None), P("src", None), P("src"))
    return jax.shard_map(
        shards,
        mesh=mesh,
        in_specs=placed,
        out_specs=(P("layer", "src", None), P("layer", "src", None)),
        check_vma=False,
    )
```

profile of v0, /device:TPU:1, one launch (start us, length us, event | category | flops | bytes accessed | tf_op | source)
XLA Modules:
  0.0 222.5 jit_solution(16298921639213100977)
XLA Ops:
  2.4 207.1 %while.20 = (s32[]{:T(128)}, f32[1,64,1664]{2,1,0:T(8,128)S(1)}, bf16[64,1664]{1,0:T(8,128)(2,1)S(1)}, f32[1,64,1664]{2,1,0:T(8,128)S(1)}, bf16[64,1664]{1,0:T(8...) while((s32[]{:T(128)}, f32[1,64,1664]{2,1,0:T(8,128)S(1)}, ...), condition=%wide.region_5.6_spmd.clone, body=%wide.region_0.5_spmd.clone.sunk | while | flops 709689344 | bytes 17891692 | solution.py:107
  2.5 4.5 %collective-permute-start = (bf16[64,1664]{1,0:T(8,128)(2,1)S(1)}, bf16[64,1664]{1,0:T(8,128)(2,1)S(1)}, u32[]{:S(2)}, u32[]{:S(2)}) collective-permute-start(bf16[64,1664]{1,0:T(8,128)(2,1)S(1)} %get-tuple-element.329), channel_id=1, source_target_pairs={{0,2},{2,4},{4,6},{6,8},{8,10},{10,12},{12,14},{14,16},{16,18},{18... | collective-permute-start | bytes 638984 | tf_op jit(solution)/shard_map/while/body/eval_jaxpr/ppermute | solution.py:10
  9.8 4.5 %collective-permute-done.1 = bf16[64,1664]{1,0:T(8,128)(2,1)S(1)} collective-permute-done((bf16[64,1664]{1,0:T(8,128)(2,1)S(1)}, bf16[64,1664]{1,0:T(8,128)(2,1)S(1)}, u32[]{:S(2)}, u32[]{:S(2)}) %collective-permute-start.1) | collective-permute-done | bytes 213024 | tf_op jit(solution)/shard_map/while/body/eval_jaxpr/ppermute | solution.py:10
  14.3 3.6 %conditional.7 = (f32[1,64,1664]{2,1,0:T(8,128)S(1)}, bf16[64,1664]{1,0:T(8,128)(2,1)S(1)}) conditional(s32[]{:T(128)} %convert_element_type.46, () %tuple.67, (f32[1,64,1664]{2,1,0:T(8,128)S(1)}, bf16[1,1664,1664]{2,1,0:T(8,128)(2,1)}, bf16[64,1664]{1,0:T(8,128)(2,1)S(1)}) %tuple.68), branch_computations={%region_1.1_spmd, %region_2.2_spmd} | conditional | flops 354631680 | bytes 6815760 | solution.py:53
  14.3 3.6 %fusion.32 = (bf16[64,1664]{1,0:T(8,128)(2,1)S(1)}, f32[64,1664]{1,0:T(8,128)S(1)}) fusion(bf16[64,1664]{1,0:T(8,128)(2,1)S(1)} %get-tuple-element.170, bf16[1,1664,1664]{2,1,0:T(8,128)(2,1)} %get-tuple-element.171, f32[1,64,1664]{2,1,0:T(8,128)S(1)} %get-tuple-element.169), kind=kOutput, calls=%fused_computation.23 | convolution fusion | flops 354631680 | bytes 6815744 | tf_op jit(solution)/shard_map/while/body/eval_jaxpr/cond/branch_1_fun/dot_general | solution.py:34
  20.0 2.4 %collective-permute-start.1 = (bf16[64,1664]{1,0:T(8,128)(2,1)S(1)}, bf16[64,1664]{1,0:T(8,128)(2,1)S(1)}, u32[]{:S(2)}, u32[]{:S(2)}) collective-permute-start(bf16[64,1664]{1,0:T(8,128)(2,1)S(1)} %get-tuple-element.331), channel_id=1, source_target_pairs={{2,0},{4,2},{6,4},{8,6},{10,8},{12,10},{14,12},{16,14},{18,16},{20... | collective-permute-start | bytes 638984 | tf_op jit(solution)/shard_map/while/body/eval_jaxpr/ppermute | solution.py:10
  22.7 4.5 %collective-permute-done.1 = bf16[64,1664]{1,0:T(8,128)(2,1)S(1)} collective-permute-done((bf16[64,1664]{1,0:T(8,128)(2,1)S(1)}, bf16[64,1664]{1,0:T(8,128)(2,1)S(1)}, u32[]{:S(2)}, u32[]{:S(2)}) %collective-permute-start.1) | collective-permute-done | bytes 213024 | tf_op jit(solution)/shard_map/while/body/eval_jaxpr/ppermute | solution.py:10
  27.2 5.8 %collective-permute-start = (bf16[64,1664]{1,0:T(8,128)(2,1)S(1)}, bf16[64,1664]{1,0:T(8,128)(2,1)S(1)}, u32[]{:S(2)}, u32[]{:S(2)}) collective-permute-start(bf16[64,1664]{1,0:T(8,128)(2,1)S(1)} %get-tuple-element.329), channel_id=1, source_target_pairs={{0,2},{2,4},{4,6},{6,8},{8,10},{10,12},{12,14},{14,16},{16,18},{18... | collective-permute-start | bytes 638984 | tf_op jit(solution)/shard_map/while/body/eval_jaxpr/ppermute | solution.py:10
  37.2 3.0 %collective-permute-done.1 = bf16[64,1664]{1,0:T(8,128)(2,1)S(1)} collective-permute-done((bf16[64,1664]{1,0:T(8,128)(2,1)S(1)}, bf16[64,1664]{1,0:T(8,128)(2,1)S(1)}, u32[]{:S(2)}, u32[]{:S(2)}) %collective-permute-start.1) | collective-permute-done | bytes 213024 | tf_op jit(solution)/shard_map/while/body/eval_jaxpr/ppermute | solution.py:10
  42.3 2.4 %collective-permute-start.1 = (bf16[64,1664]{1,0:T(8,128)(2,1)S(1)}, bf16[64,1664]{1,0:T(8,128)(2,1)S(1)}, u32[]{:S(2)}, u32[]{:S(2)}) collective-permute-start(bf16[64,1664]{1,0:T(8,128)(2,1)S(1)} %get-tuple-element.331), channel_id=1, source_target_pairs={{2,0},{4,2},{6,4},{8,6},{10,8},{12,10},{14,12},{16,14},{18,16},{20... | collective-permute-start | bytes 638984 | tf_op jit(solution)/shard_map/while/body/eval_jaxpr/ppermute | solution.py:10
  45.0 4.5 %collective-permute-done.1 = bf16[64,1664]{1,0:T(8,128)(2,1)S(1)} collective-permute-done((bf16[64,1664]{1,0:T(8,128)(2,1)S(1)}, bf16[64,1664]{1,0:T(8,128)(2,1)S(1)}, u32[]{:S(2)}, u32[]{:S(2)}) %collective-permute-start.1) | collective-permute-done | bytes 213024 | tf_op jit(solution)/shard_map/while/body/eval_jaxpr/ppermute | solution.py:10
  51.6 2.4 %collective-permute-start.1 = (bf16[64,1664]{1,0:T(8,128)(2,1)S(1)}, bf16[64,1664]{1,0:T(8,128)(2,1)S(1)}, u32[]{:S(2)}, u32[]{:S(2)}) collective-permute-start(bf16[64,1664]{1,0:T(8,128)(2,1)S(1)} %get-tuple-element.331), channel_id=1, source_target_pairs={{2,0},{4,2},{6,4},{8,6},{10,8},{12,10},{14,12},{16,14},{18,16},{20... | collective-permute-start | bytes 638984 | tf_op jit(solution)/shard_map/while/body/eval_jaxpr/ppermute | solution.py:10
  54.3 4.5 %collective-permute-done.1 = bf16[64,1664]{1,0:T(8,128)(2,1)S(1)} collective-permute-done((bf16[64,1664]{1,0:T(8,128)(2,1)S(1)}, bf16[64,1664]{1,0:T(8,128)(2,1)S(1)}, u32[]{:S(2)}, u32[]{:S(2)}) %collective-permute-start.1) | collective-permute-done | bytes 213024 | tf_op jit(solution)/shard_map/while/body/eval_jaxpr/ppermute | solution.py:10
  58.8 2.6 %collective-permute-start = (bf16[64,1664]{1,0:T(8,128)(2,1)S(1)}, bf16[64,1664]{1,0:T(8,128)(2,1)S(1)}, u32[]{:S(2)}, u32[]{:S(2)}) collective-permute-start(bf16[64,1664]{1,0:T(8,128)(2,1)S(1)} %get-tuple-element.329), channel_id=1, source_target_pairs={{0,2},{2,4},{4,6},{6,8},{8,10},{10,12},{12,14},{14,16},{16,18},{18... | collective-permute-start | bytes 638984 | tf_op jit(solution)/shard_map/while/body/eval_jaxpr/ppermute | solution.py:10
  64.6 7.6 %collective-permute-done.1 = bf16[64,1664]{1,0:T(8,128)(2,1)S(1)} collective-permute-done((bf16[64,1664]{1,0:T(8,128)(2,1)S(1)}, bf16[64,1664]{1,0:T(8,128)(2,1)S(1)}, u32[]{:S(2)}, u32[]{:S(2)}) %collective-permute-start.1) | collective-permute-done | bytes 213024 | tf_op jit(solution)/shard_map/while/body/eval_jaxpr/ppermute | solution.py:10
  77.0 5.4 %collective-permute-done.1 = bf16[64,1664]{1,0:T(8,128)(2,1)S(1)} collective-permute-done((bf16[64,1664]{1,0:T(8,128)(2,1)S(1)}, bf16[64,1664]{1,0:T(8,128)(2,1)S(1)}, u32[]{:S(2)}, u32[]{:S(2)}) %collective-permute-start.1) | collective-permute-done | bytes 213024 | tf_op jit(solution)/shard_map/while/body/eval_jaxpr/ppermute | solution.py:10
  84.4 2.4 %collective-permute-start.1 = (bf16[64,1664]{1,0:T(8,128)(2,1)S(1)}, bf16[64,1664]{1,0:T(8,128)(2,1)S(1)}, u32[]{:S(2)}, u32[]{:S(2)}) collective-permute-start(bf16[64,1664]{1,0:T(8,128)(2,1)S(1)} %get-tuple-element.331), channel_id=1, source_target_pairs={{2,0},{4,2},{6,4},{8,6},{10,8},{12,10},{14,12},{16,14},{18,16},{20... | collective-permute-start | bytes 638984 | tf_op jit(solution)/shard_map/while/body/eval_jaxpr/ppermute | solution.py:10
  87.1 5.4 %collective-permute-done.1 = bf16[64,1664]{1,0:T(8,128)(2,1)S(1)} collective-permute-done((bf16[64,1664]{1,0:T(8,128)(2,1)S(1)}, bf16[64,1664]{1,0:T(8,128)(2,1)S(1)}, u32[]{:S(2)}, u32[]{:S(2)}) %collective-permute-start.1) | collective-permute-done | bytes 213024 | tf_op jit(solution)/shard_map/while/body/eval_jaxpr/ppermute | solution.py:10
  97.3 5.4 %collective-permute-done.1 = bf16[64,1664]{1,0:T(8,128)(2,1)S(1)} collective-permute-done((bf16[64,1664]{1,0:T(8,128)(2,1)S(1)}, bf16[64,1664]{1,0:T(8,128)(2,1)S(1)}, u32[]{:S(2)}, u32[]{:S(2)}) %collective-permute-start.1) | collective-permute-done | bytes 213024 | tf_op jit(solution)/shard_map/while/body/eval_jaxpr/ppermute | solution.py:10
  107.4 13.0 %collective-permute-done.1 = bf16[64,1664]{1,0:T(8,128)(2,1)S(1)} collective-permute-done((bf16[64,1664]{1,0:T(8,128)(2,1)S(1)}, bf16[64,1664]{1,0:T(8,128)(2,1)S(1)}, u32[]{:S(2)}, u32[]{:S(2)}) %collective-permute-start.1) | collective-permute-done | bytes 213024 | tf_op jit(solution)/shard_map/while/body/eval_jaxpr/ppermute | solution.py:10
  125.2 7.5 %collective-permute-done.1 = bf16[64,1664]{1,0:T(8,128)(2,1)S(1)} collective-permute-done((bf16[64,1664]{1,0:T(8,128)(2,1)S(1)}, bf16[64,1664]{1,0:T(8,128)(2,1)S(1)}, u32[]{:S(2)}, u32[]{:S(2)}) %collective-permute-start.1) | collective-permute-done | bytes 213024 | tf_op jit(solution)/shard_map/while/body/eval_jaxpr/ppermute | solution.py:10
  137.5 16.0 %collective-permute-done.1 = bf16[64,1664]{1,0:T(8,128)(2,1)S(1)} collective-permute-done((bf16[64,1664]{1,0:T(8,128)(2,1)S(1)}, bf16[64,1664]{1,0:T(8,128)(2,1)S(1)}, u32[]{:S(2)}, u32[]{:S(2)}) %collective-permute-start.1) | collective-permute-done | bytes 213024 | tf_op jit(solution)/shard_map/while/body/eval_jaxpr/ppermute | solution.py:10
  160.5 9.5 %collective-permute-done.1 = bf16[64,1664]{1,0:T(8,128)(2,1)S(1)} collective-permute-done((bf16[64,1664]{1,0:T(8,128)(2,1)S(1)}, bf16[64,1664]{1,0:T(8,128)(2,1)S(1)}, u32[]{:S(2)}, u32[]{:S(2)}) %collective-permute-start.1) | collective-permute-done | bytes 213024 | tf_op jit(solution)/shard_map/while/body/eval_jaxpr/ppermute | solution.py:10
  170.1 2.9 %collective-permute-start = (bf16[64,1664]{1,0:T(8,128)(2,1)S(1)}, bf16[64,1664]{1,0:T(8,128)(2,1)S(1)}, u32[]{:S(2)}, u32[]{:S(2)}) collective-permute-start(bf16[64,1664]{1,0:T(8,128)(2,1)S(1)} %get-tuple-element.329), channel_id=1, source_target_pairs={{0,2},{2,4},{4,6},{6,8},{8,10},{10,12},{12,14},{14,16},{16,18},{18... | collective-permute-start | bytes 638984 | tf_op jit(solution)/shard_map/while/body/eval_jaxpr/ppermute | solution.py:10
  176.2 11.2 %collective-permute-done.1 = bf16[64,1664]{1,0:T(8,128)(2,1)S(1)} collective-permute-done((bf16[64,1664]{1,0:T(8,128)(2,1)S(1)}, bf16[64,1664]{1,0:T(8,128)(2,1)S(1)}, u32[]{:S(2)}, u32[]{:S(2)}) %collective-permute-start.1) | collective-permute-done | bytes 213024 | tf_op jit(solution)/shard_map/while/body/eval_jaxpr/ppermute | solution.py:10
  189.4 3.7 %conditional.6 = (f32[1,64,1664]{2,1,0:T(8,128)S(1)}, bf16[64,1664]{1,0:T(8,128)(2,1)S(1)}) conditional(s32[]{:T(128)} %convert_element_type.45, () %tuple.65, (f32[1,64,1664]{2,1,0:T(8,128)S(1)}, bf16[1,1664,1664]{2,1,0:T(8,128)(2,1)}, bf16[64,1664]{1,0:T(8,128)(2,1)S(1)}) %tuple.66), branch_computations={%region_3.3_spmd, %region_4.4_spmd} | conditional | flops 354631680 | bytes 6815760 | solution.py:53
  189.4 3.6 %fusion.33 = (bf16[64,1664]{1,0:T(8,128)(2,1)S(1)}, f32[64,1664]{1,0:T(8,128)S(1)}) fusion(bf16[64,1664]{1,0:T(8,128)(2,1)S(1)} %get-tuple-element.173, bf16[1,1664,1664]{2,1,0:T(8,128)(2,1)} %get-tuple-element.174, f32[1,64,1664]{2,1,0:T(8,128)S(1)} %get-tuple-element.172), kind=kOutput, calls=%fused_computation.24 | convolution fusion | flops 354631680 | bytes 6815744 | tf_op jit(solution)/shard_map/while/body/eval_jaxpr/cond/branch_1_fun/dot_general | solution.py:34
  195.3 5.0 %collective-permute-done.1 = bf16[64,1664]{1,0:T(8,128)(2,1)S(1)} collective-permute-done((bf16[64,1664]{1,0:T(8,128)(2,1)S(1)}, bf16[64,1664]{1,0:T(8,128)(2,1)S(1)}, u32[]{:S(2)}, u32[]{:S(2)}) %collective-permute-start.1) | collective-permute-done | bytes 213024 | tf_op jit(solution)/shard_map/while/body/eval_jaxpr/ppermute | solution.py:10
  202.3 6.0 %collective-permute-start.1 = (bf16[64,1664]{1,0:T(8,128)(2,1)S(1)}, bf16[64,1664]{1,0:T(8,128)(2,1)S(1)}, u32[]{:S(2)}, u32[]{:S(2)}) collective-permute-start(bf16[64,1664]{1,0:T(8,128)(2,1)S(1)} %get-tuple-element.331), channel_id=1, source_target_pairs={{2,0},{4,2},{6,4},{8,6},{10,8},{12,10},{14,12},{16,14},{18,16},{20... | collective-permute-start | bytes 638984 | tf_op jit(solution)/shard_map/while/body/eval_jaxpr/ppermute | solution.py:10
  209.6 2.5 %collective-permute-start.3 = (bf16[1,64,1664]{2,1,0:T(8,128)(2,1)S(1)}, bf16[1,64,1664]{2,1,0:T(8,128)(2,1)S(1)}, u32[]{:S(2)}, u32[]{:S(2)}) collective-permute-start(bf16[1,64,1664]{2,1,0:T(8,128)(2,1)S(1)} %fusion.31), channel_id=1, source_target_pairs={{2,0},{4,2},{6,4},{8,6},{10,8},{12,10},{14,12},{16,14},{18,16},{20... | collective-permute-start | bytes 638984 | tf_op jit(solution)/shard_map/ppermute | solution.py:23
  212.1 3.4 %collective-permute-start.2 = (bf16[1,64,1664]{2,1,0:T(8,128)(2,1)S(1)}, bf16[1,64,1664]{2,1,0:T(8,128)(2,1)S(1)}, u32[]{:S(2)}, u32[]{:S(2)}) collective-permute-start(bf16[1,64,1664]{2,1,0:T(8,128)(2,1)S(1)} %fusion.31), channel_id=1, source_target_pairs={{0,2},{2,4},{4,6},{6,8},{8,10},{10,12},{12,14},{14,16},{16,18},{18... | collective-permute-start | bytes 638984 | tf_op jit(solution)/shard_map/ppermute | solution.py:21
  217.1 3.6 %fusion.17 = f32[1,64,1664]{2,1,0:T(8,128)S(1)} fusion(bf16[1,1664,1664]{2,1,0:T(8,128)(2,1)} %get-tuple-element.376, bf16[1,64,1664]{2,1,0:T(8,128)(2,1)S(1)} %collective-permute-done.3), kind=kOutput, calls=%fused_computation.13 | convolution fusion | flops 354418688 | bytes 6176768 | tf_op jit(solution)/shard_map/lsw,lwv->lsv/dot_general | solution.py:116
  (162 shorter events, 67.3 us)
Async XLA Ops:
  2.5 7.3 %collective-permute-start = (bf16[64,1664]{1,0:T(8,128)(2,1)S(1)}, bf16[64,1664]{1,0:T(8,128)(2,1)S(1)}, u32[]{:S(2)}, u32[]{:S(2)}) collective-permute-start(bf16[64,1664]{1,0:T(8,128)(2,1)S(1)} %get-tuple-element.329), channel_id=1, source_target_pairs={{0,2},{2,4},{4,6},{6,8},{8,10},{10,12},{12,14},{14,16},{16,18},{18... | collective-permute-start | bytes 638984 | tf_op jit(solution)/shard_map/while/body/eval_jaxpr/ppermute | solution.py:10
  7.1 7.2 %collective-permute-start.1 = (bf16[64,1664]{1,0:T(8,128)(2,1)S(1)}, bf16[64,1664]{1,0:T(8,128)(2,1)S(1)}, u32[]{:S(2)}, u32[]{:S(2)}) collective-permute-start(bf16[64,1664]{1,0:T(8,128)(2,1)S(1)} %get-tuple-element.331), channel_id=1, source_target_pairs={{2,0},{4,2},{6,4},{8,6},{10,8},{12,10},{14,12},{16,14},{18,16},{20... | collective-permute-start | bytes 638984 | tf_op jit(solution)/shard_map/while/body/eval_jaxpr/ppermute | solution.py:10
  17.9 4.7 %collective-permute-start = (bf16[64,1664]{1,0:T(8,128)(2,1)S(1)}, bf16[64,1664]{1,0:T(8,128)(2,1)S(1)}, u32[]{:S(2)}, u32[]{:S(2)}) collective-permute-start(bf16[64,1664]{1,0:T(8,128)(2,1)S(1)} %get-tuple-element.329), channel_id=1, source_target_pairs={{0,2},{2,4},{4,6},{6,8},{8,10},{10,12},{12,14},{14,16},{16,18},{18... | collective-permute-start | bytes 638984 | tf_op jit(solution)/shard_map/while/body/eval_jaxpr/ppermute | solution.py:10
  20.0 7.2 %collective-permute-start.1 = (bf16[64,1664]{1,0:T(8,128)(2,1)S(1)}, bf16[64,1664]{1,0:T(8,128)(2,1)S(1)}, u32[]{:S(2)}, u32[]{:S(2)}) collective-permute-start(bf16[64,1664]{1,0:T(8,128)(2,1)S(1)} %get-tuple-element.331), channel_id=1, source_target_pairs={{2,0},{4,2},{6,4},{8,6},{10,8},{12,10},{14,12},{16,14},{18,16},{20... | collective-permute-start | bytes 638984 | tf_op jit(solution)/shard_map/while/body/eval_jaxpr/ppermute | solution.py:10
  27.2 10.0 %collective-permute-start = (bf16[64,1664]{1,0:T(8,128)(2,1)S(1)}, bf16[64,1664]{1,0:T(8,128)(2,1)S(1)}, u32[]{:S(2)}, u32[]{:S(2)}) collective-permute-start(bf16[64,1664]{1,0:T(8,128)(2,1)S(1)} %get-tuple-element.329), channel_id=1, source_target_pairs={{0,2},{2,4},{4,6},{6,8},{8,10},{10,12},{12,14},{14,16},{16,18},{18... | collective-permute-start | bytes 638984 | tf_op jit(solution)/shard_map/while/body/eval_jaxpr/ppermute | solution.py:10
  33.1 7.2 %collective-permute-start.1 = (bf16[64,1664]{1,0:T(8,128)(2,1)S(1)}, bf16[64,1664]{1,0:T(8,128)(2,1)S(1)}, u32[]{:S(2)}, u32[]{:S(2)}) collective-permute-start(bf16[64,1664]{1,0:T(8,128)(2,1)S(1)} %get-tuple-element.331), channel_id=1, source_target_pairs={{2,0},{4,2},{6,4},{8,6},{10,8},{12,10},{14,12},{16,14},{18,16},{20... | collective-permute-start | bytes 638984 | tf_op jit(solution)/shard_map/while/body/eval_jaxpr/ppermute | solution.py:10
  40.3 4.7 %collective-permute-start = (bf16[64,1664]{1,0:T(8,128)(2,1)S(1)}, bf16[64,1664]{1,0:T(8,128)(2,1)S(1)}, u32[]{:S(2)}, u32[]{:S(2)}) collective-permute-start(bf16[64,1664]{1,0:T(8,128)(2,1)S(1)} %get-tuple-element.329), channel_id=1, source_target_pairs={{0,2},{2,4},{4,6},{6,8},{8,10},{10,12},{12,14},{14,16},{16,18},{18... | collective-permute-start | bytes 638984 | tf_op jit(solution)/shard_map/while/body/eval_jaxpr/ppermute | solution.py:10
  42.3 7.2 %collective-permute-start.1 = (bf16[64,1664]{1,0:T(8,128)(2,1)S(1)}, bf16[64,1664]{1,0:T(8,128)(2,1)S(1)}, u32[]{:S(2)}, u32[]{:S(2)}) collective-permute-start(bf16[64,1664]{1,0:T(8,128)(2,1)S(1)} %get-tuple-element.331), channel_id=1, source_target_pairs={{2,0},{4,2},{6,4},{8,6},{10,8},{12,10},{14,12},{16,14},{18,16},{20... | collective-permute-start | bytes 638984 | tf_op jit(solution)/shard_map/while/body/eval_jaxpr/ppermute | solution.py:10
  49.5 4.7 %collective-permute-start = (bf16[64,1664]{1,0:T(8,128)(2,1)S(1)}, bf16[64,1664]{1,0:T(8,128)(2,1)S(1)}, u32[]{:S(2)}, u32[]{:S(2)}) collective-permute-start(bf16[64,1664]{1,0:T(8,128)(2,1)S(1)} %get-tuple-element.329), channel_id=1, source_target_pairs={{0,2},{2,4},{4,6},{6,8},{8,10},{10,12},{12,14},{14,16},{16,18},{18... | collective-permute-start | bytes 638984 | tf_op jit(solution)/shard_map/while/body/eval_jaxpr/ppermute | solution.py:10
  51.6 7.2 %collective-permute-start.1 = (bf16[64,1664]{1,0:T(8,128)(2,1)S(1)}, bf16[64,1664]{1,0:T(8,128)(2,1)S(1)}, u32[]{:S(2)}, u32[]{:S(2)}) collective-permute-start(bf16[64,1664]{1,0:T(8,128)(2,1)S(1)} %get-tuple-element.331), channel_id=1, source_target_pairs={{2,0},{4,2},{6,4},{8,6},{10,8},{12,10},{14,12},{16,14},{18,16},{20... | collective-permute-start | bytes 638984 | tf_op jit(solution)/shard_map/while/body/eval_jaxpr/ppermute | solution.py:10
  58.8 5.8 %collective-permute-start = (bf16[64,1664]{1,0:T(8,128)(2,1)S(1)}, bf16[64,1664]{1,0:T(8,128)(2,1)S(1)}, u32[]{:S(2)}, u32[]{:S(2)}) collective-permute-start(bf16[64,1664]{1,0:T(8,128)(2,1)S(1)} %get-tuple-element.329), channel_id=1, source_target_pairs={{0,2},{2,4},{4,6},{6,8},{8,10},{10,12},{12,14},{14,16},{16,18},{18... | collective-permute-start | bytes 638984 | tf_op jit(solution)/shard_map/while/body/eval_jaxpr/ppermute | solution.py:10
  61.5 10.7 %collective-permute-start.1 = (bf16[64,1664]{1,0:T(8,128)(2,1)S(1)}, bf16[64,1664]{1,0:T(8,128)(2,1)S(1)}, u32[]{:S(2)}, u32[]{:S(2)}) collective-permute-start(bf16[64,1664]{1,0:T(8,128)(2,1)S(1)} %get-tuple-element.331), channel_id=1, source_target_pairs={{2,0},{4,2},{6,4},{8,6},{10,8},{12,10},{14,12},{16,14},{18,16},{20... | collective-permute-start | bytes 638984 | tf_op jit(solution)/shard_map/while/body/eval_jaxpr/ppermute | solution.py:10
  72.3 4.7 %collective-permute-start = (bf16[64,1664]{1,0:T(8,128)(2,1)S(1)}, bf16[64,1664]{1,0:T(8,128)(2,1)S(1)}, u32[]{:S(2)}, u32[]{:S(2)}) collective-permute-start(bf16[64,1664]{1,0:T(8,128)(2,1)S(1)} %get-tuple-element.329), channel_id=1, source_target_pairs={{0,2},{2,4},{4,6},{6,8},{8,10},{10,12},{12,14},{14,16},{16,18},{18... | collective-permute-start | bytes 638984 | tf_op jit(solution)/shard_map/while/body/eval_jaxpr/ppermute | solution.py:10
  74.3 8.1 %collective-permute-start.1 = (bf16[64,1664]{1,0:T(8,128)(2,1)S(1)}, bf16[64,1664]{1,0:T(8,128)(2,1)S(1)}, u32[]{:S(2)}, u32[]{:S(2)}) collective-permute-start(bf16[64,1664]{1,0:T(8,128)(2,1)S(1)} %get-tuple-element.331), channel_id=1, source_target_pairs={{2,0},{4,2},{6,4},{8,6},{10,8},{12,10},{14,12},{16,14},{18,16},{20... | collective-permute-start | bytes 638984 | tf_op jit(solution)/shard_map/while/body/eval_jaxpr/ppermute | solution.py:10
  82.4 4.7 %collective-permute-start = (bf16[64,1664]{1,0:T(8,128)(2,1)S(1)}, bf16[64,1664]{1,0:T(8,128)(2,1)S(1)}, u32[]{:S(2)}, u32[]{:S(2)}) collective-permute-start(bf16[64,1664]{1,0:T(8,128)(2,1)S(1)} %get-tuple-element.329), channel_id=1, source_target_pairs={{0,2},{2,4},{4,6},{6,8},{8,10},{10,12},{12,14},{14,16},{16,18},{18... | collective-permute-start | bytes 638984 | tf_op jit(solution)/shard_map/while/body/eval_jaxpr/ppermute | solution.py:10
  84.4 8.1 %collective-permute-start.1 = (bf16[64,1664]{1,0:T(8,128)(2,1)S(1)}, bf16[64,1664]{1,0:T(8,128)(2,1)S(1)}, u32[]{:S(2)}, u32[]{:S(2)}) collective-permute-start(bf16[64,1664]{1,0:T(8,128)(2,1)S(1)} %get-tuple-element.331), channel_id=1, source_target_pairs={{2,0},{4,2},{6,4},{8,6},{10,8},{12,10},{14,12},{16,14},{18,16},{20... | collective-permute-start | bytes 638984 | tf_op jit(solution)/shard_map/while/body/eval_jaxpr/ppermute | solution.py:10
  92.6 4.7 %collective-permute-start = (bf16[64,1664]{1,0:T(8,128)(2,1)S(1)}, bf16[64,1664]{1,0:T(8,128)(2,1)S(1)}, u32[]{:S(2)}, u32[]{:S(2)}) collective-permute-start(bf16[64,1664]{1,0:T(8,128)(2,1)S(1)} %get-tuple-element.329), channel_id=1, source_target_pairs={{0,2},{2,4},{4,6},{6,8},{8,10},{10,12},{12,14},{14,16},{16,18},{18... | collective-permute-start | bytes 638984 | tf_op jit(solution)/shard_map/while/body/eval_jaxpr/ppermute | solution.py:10
  94.6 8.1 %collective-permute-start.1 = (bf16[64,1664]{1,0:T(8,128)(2,1)S(1)}, bf16[64,1664]{1,0:T(8,128)(2,1)S(1)}, u32[]{:S(2)}, u32[]{:S(2)}) collective-permute-start(bf16[64,1664]{1,0:T(8,128)(2,1)S(1)} %get-tuple-element.331), channel_id=1, source_target_pairs={{2,0},{4,2},{6,4},{8,6},{10,8},{12,10},{14,12},{16,14},{18,16},{20... | collective-permute-start | bytes 638984 | tf_op jit(solution)/shard_map/while/body/eval_jaxpr/ppermute | solution.py:10
  104.7 15.7 %collective-permute-start.1 = (bf16[64,1664]{1,0:T(8,128)(2,1)S(1)}, bf16[64,1664]{1,0:T(8,128)(2,1)S(1)}, u32[]{:S(2)}, u32[]{:S(2)}) collective-permute-start(bf16[64,1664]{1,0:T(8,128)(2,1)S(1)} %get-tuple-element.331), channel_id=1, source_target_pairs={{2,0},{4,2},{6,4},{8,6},{10,8},{12,10},{14,12},{16,14},{18,16},{20... | collective-permute-start | bytes 638984 | tf_op jit(solution)/shard_map/while/body/eval_jaxpr/ppermute | solution.py:10
  120.5 4.7 %collective-permute-start = (bf16[64,1664]{1,0:T(8,128)(2,1)S(1)}, bf16[64,1664]{1,0:T(8,128)(2,1)S(1)}, u32[]{:S(2)}, u32[]{:S(2)}) collective-permute-start(bf16[64,1664]{1,0:T(8,128)(2,1)S(1)} %get-tuple-element.329), channel_id=1, source_target_pairs={{0,2},{2,4},{4,6},{6,8},{8,10},{10,12},{12,14},{14,16},{16,18},{18... | collective-permute-start | bytes 638984 | tf_op jit(solution)/shard_map/while/body/eval_jaxpr/ppermute | solution.py:10
  122.5 10.2 %collective-permute-start.1 = (bf16[64,1664]{1,0:T(8,128)(2,1)S(1)}, bf16[64,1664]{1,0:T(8,128)(2,1)S(1)}, u32[]{:S(2)}, u32[]{:S(2)}) collective-permute-start(bf16[64,1664]{1,0:T(8,128)(2,1)S(1)} %get-tuple-element.331), channel_id=1, source_target_pairs={{2,0},{4,2},{6,4},{8,6},{10,8},{12,10},{14,12},{16,14},{18,16},{20... | collective-permute-start | bytes 638984 | tf_op jit(solution)/shard_map/while/body/eval_jaxpr/ppermute | solution.py:10
  134.8 18.7 %collective-permute-start.1 = (bf16[64,1664]{1,0:T(8,128)(2,1)S(1)}, bf16[64,1664]{1,0:T(8,128)(2,1)S(1)}, u32[]{:S(2)}, u32[]{:S(2)}) collective-permute-start(bf16[64,1664]{1,0:T(8,128)(2,1)S(1)} %get-tuple-element.331), channel_id=1, source_target_pairs={{2,0},{4,2},{6,4},{8,6},{10,8},{12,10},{14,12},{16,14},{18,16},{20... | collective-permute-start | bytes 638984 | tf_op jit(solution)/shard_map/while/body/eval_jaxpr/ppermute | solution.py:10
  153.5 7.0 %collective-permute-start = (bf16[64,1664]{1,0:T(8,128)(2,1)S(1)}, bf16[64,1664]{1,0:T(8,128)(2,1)S(1)}, u32[]{:S(2)}, u32[]{:S(2)}) collective-permute-start(bf16[64,1664]{1,0:T(8,128)(2,1)S(1)} %get-tuple-element.329), channel_id=1, source_target_pairs={{0,2},{2,4},{4,6},{6,8},{8,10},{10,12},{12,14},{14,16},{16,18},{18... | collective-permute-start | bytes 638984 | tf_op jit(solution)/shard_map/while/body/eval_jaxpr/ppermute | solution.py:10
  155.6 14.5 %collective-permute-start.1 = (bf16[64,1664]{1,0:T(8,128)(2,1)S(1)}, bf16[64,1664]{1,0:T(8,128)(2,1)S(1)}, u32[]{:S(2)}, u32[]{:S(2)}) collective-permute-start(bf16[64,1664]{1,0:T(8,128)(2,1)S(1)} %get-tuple-element.331), channel_id=1, source_target_pairs={{2,0},{4,2},{6,4},{8,6},{10,8},{12,10},{14,12},{16,14},{18,16},{20... | collective-permute-start | bytes 638984 | tf_op jit(solution)/shard_map/while/body/eval_jaxpr/ppermute | solution.py:10
  170.1 6.2 %collective-permute-start = (bf16[64,1664]{1,0:T(8,128)(2,1)S(1)}, bf16[64,1664]{1,0:T(8,128)(2,1)S(1)}, u32[]{:S(2)}, u32[]{:S(2)}) collective-permute-start(bf16[64,1664]{1,0:T(8,128)(2,1)S(1)} %get-tuple-element.329), channel_id=1, source_target_pairs={{0,2},{2,4},{4,6},{6,8},{8,10},{10,12},{12,14},{14,16},{16,18},{18... | collective-permute-start | bytes 638984 | tf_op jit(solution)/shard_map/while/body/eval_jaxpr/ppermute | solution.py:10
  173.1 14.3 %collective-permute-start.1 = (bf16[64,1664]{1,0:T(8,128)(2,1)S(1)}, bf16[64,1664]{1,0:T(8,128)(2,1)S(1)}, u32[]{:S(2)}, u32[]{:S(2)}) collective-permute-start(bf16[64,1664]{1,0:T(8,128)(2,1)S(1)} %get-tuple-element.331), channel_id=1, source_target_pairs={{2,0},{4,2},{6,4},{8,6},{10,8},{12,10},{14,12},{16,14},{18,16},{20... | collective-permute-start | bytes 638984 | tf_op jit(solution)/shard_map/while/body/eval_jaxpr/ppermute | solution.py:10
  187.5 7.8 %collective-permute-start = (bf16[64,1664]{1,0:T(8,128)(2,1)S(1)}, bf16[64,1664]{1,0:T(8,128)(2,1)S(1)}, u32[]{:S(2)}, u32[]{:S(2)}) collective-permute-start(bf16[64,1664]{1,0:T(8,128)(2,1)S(1)} %get-tuple-element.329), channel_id=1, source_target_pairs={{0,2},{2,4},{4,6},{6,8},{8,10},{10,12},{12,14},{14,16},{16,18},{18... | collective-permute-start | bytes 638984 | tf_op jit(solution)/shard_map/while/body/eval_jaxpr/ppermute | solution.py:10
  193.1 7.2 %collective-permute-start.1 = (bf16[64,1664]{1,0:T(8,128)(2,1)S(1)}, bf16[64,1664]{1,0:T(8,128)(2,1)S(1)}, u32[]{:S(2)}, u32[]{:S(2)}) collective-permute-start(bf16[64,1664]{1,0:T(8,128)(2,1)S(1)} %get-tuple-element.331), channel_id=1, source_target_pairs={{2,0},{4,2},{6,4},{8,6},{10,8},{12,10},{14,12},{16,14},{18,16},{20... | collective-permute-start | bytes 638984 | tf_op jit(solution)/shard_map/while/body/eval_jaxpr/ppermute | solution.py:10
  200.3 8.3 %collective-permute-start = (bf16[64,1664]{1,0:T(8,128)(2,1)S(1)}, bf16[64,1664]{1,0:T(8,128)(2,1)S(1)}, u32[]{:S(2)}, u32[]{:S(2)}) collective-permute-start(bf16[64,1664]{1,0:T(8,128)(2,1)S(1)} %get-tuple-element.329), channel_id=1, source_target_pairs={{0,2},{2,4},{4,6},{6,8},{8,10},{10,12},{12,14},{14,16},{16,18},{18... | collective-permute-start | bytes 638984 | tf_op jit(solution)/shard_map/while/body/eval_jaxpr/ppermute | solution.py:10
  202.3 7.2 %collective-permute-start.1 = (bf16[64,1664]{1,0:T(8,128)(2,1)S(1)}, bf16[64,1664]{1,0:T(8,128)(2,1)S(1)}, u32[]{:S(2)}, u32[]{:S(2)}) collective-permute-start(bf16[64,1664]{1,0:T(8,128)(2,1)S(1)} %get-tuple-element.331), channel_id=1, source_target_pairs={{2,0},{4,2},{6,4},{8,6},{10,8},{12,10},{14,12},{16,14},{18,16},{20... | collective-permute-start | bytes 638984 | tf_op jit(solution)/shard_map/while/body/eval_jaxpr/ppermute | solution.py:10
  209.6 7.4 %collective-permute-start.3 = (bf16[1,64,1664]{2,1,0:T(8,128)(2,1)S(1)}, bf16[1,64,1664]{2,1,0:T(8,128)(2,1)S(1)}, u32[]{:S(2)}, u32[]{:S(2)}) collective-permute-start(bf16[1,64,1664]{2,1,0:T(8,128)(2,1)S(1)} %fusion.31), channel_id=1, source_target_pairs={{2,0},{4,2},{6,4},{8,6},{10,8},{12,10},{14,12},{16,14},{18,16},{20... | collective-permute-start | bytes 638984 | tf_op jit(solution)/shard_map/ppermute | solution.py:23
  212.1 8.6 %collective-permute-start.2 = (bf16[1,64,1664]{2,1,0:T(8,128)(2,1)S(1)}, bf16[1,64,1664]{2,1,0:T(8,128)(2,1)S(1)}, u32[]{:S(2)}, u32[]{:S(2)}) collective-permute-start(bf16[1,64,1664]{2,1,0:T(8,128)(2,1)S(1)} %fusion.31), channel_id=1, source_target_pairs={{0,2},{2,4},{4,6},{6,8},{8,10},{10,12},{12,14},{14,16},{16,18},{18... | collective-permute-start | bytes 638984 | tf_op jit(solution)/shard_map/ppermute | solution.py:21
  (5 other events, 240.7 us)
where the time goes:
time: 224 us; the launch traced here: 223 us
  waiting for transfers between devices  115 us (51%)
  starting transfers between devices  84.9 us (38%)
  matrix products  12.7 us (6%)
  other arithmetic  5.94 us (3%)
    ppermute x32, waiting for transfers between devices, shifted(): return lax.ppermute(shard, axis, pairs)  113 us
    ppermute x32, starting transfers between devices, shifted(): return lax.ppermute(shard, axis, pairs)  79.1 us
    dot_general x2, matrix products, apply_stack(): jnp.dot(current, maps[position], preferred_element_type=jnp.float32)  7.29 us
  transfers between devices with their start and end apart: 34, of which 21 were waited for; matrix products, arithmetic and copies ran while one was open for 5% of the time, Pallas kernels for 0%

commit v1 on v0

v1 whole, which is shorter than its diff:
```python
import functools

import jax
import jax.numpy as jnp
from jax import lax
from jax.experimental import pallas as pl
from jax.experimental.pallas import tpu as pltpu
from jax.sharding import PartitionSpec as P

MESH = pl.DeviceIdType.MESH
BATCHES = 4


def kernel(
    n, batches, down_ref, up_ref, local_ref, depth_ref, traces_ref, residual_ref,
    maps, inbox, outbox, sidebox, acc, load_sem, wave_send, wave_recv, side_send, side_recv,
):
    me = lax.axis_index("layer")
    rows = inbox.shape[2]
    has_prev = me > 0
    has_next = me < n - 1
    first = jnp.where(me * 2 < n, 0, 1)

    def load(d):
        return pltpu.make_async_copy(
            (down_ref, up_ref)[d].at[0], maps.at[d], load_sem.at[d]
        )

    @pl.when(first == 0)
    def _():
        load(0).start()
        load(1).start()

    @pl.when(first == 1)
    def _():
        load(1).start()
        load(0).start()

    acc[...] = jnp.zeros_like(acc)
    barrier = pltpu.get_barrier_semaphore()

    @pl.when(has_prev)
    def _():
        pl.semaphore_signal(barrier, inc=1, device_id={"layer": me - 1}, device_id_type=MESH)

    @pl.when(has_next)
    def _():
        pl.semaphore_signal(barrier, inc=1, device_id={"layer": me + 1}, device_id_type=MESH)

    pl.semaphore_wait(barrier, has_prev.astype(jnp.int32) + has_next.astype(jnp.int32))

    def batch_rows(b):
        return pl.ds(pl.multiple_of(b * rows, rows), rows)

    def forcing(b):
        where = depth_ref[batch_rows(b), :] == me
        return jnp.where(where, local_ref[batch_rows(b), :].astype(jnp.float32), 0.0)

    def wave_copy(d, b, to):
        return pltpu.make_async_remote_copy(
            src_ref=outbox.at[d, b], dst_ref=inbox.at[d, b],
            send_sem=wave_send.at[d, b], recv_sem=wave_recv.at[d, b],
            device_id={"layer": to}, device_id_type=MESH,
        )

    def side_copy(d, b, to):
        return pltpu.make_async_remote_copy(
            src_ref=outbox.at[d, b], dst_ref=sidebox.at[d, b],
            send_sem=side_send.at[d, b], recv_sem=side_recv.at[d, b],
            device_id={"layer": to}, device_id_type=MESH,
        )

    def neighbours(d):
        step = 1 - 2 * d
        source, target = me - step, me + step
        has_source = jnp.logical_and(source >= 0, source < n)
        has_target = jnp.logical_and(target >= 0, target < n)
        return source, target, has_source, has_target

    def phase(p, carry):
        d = (first + p) % 2
        source, target, has_source, has_target = neighbours(d)
        pltpu.make_async_copy(down_ref.at[0], maps.at[d], load_sem.at[d]).wait()

        def batch(b, carry):
            @pl.when(has_source)
            def _():
                wave_copy(d, b, target).wait_recv()
                moved = jnp.dot(inbox[d, b], maps[d], preferred_element_type=jnp.float32)
                outbox[d, b] = (forcing(b) + moved).astype(jnp.bfloat16)

            @pl.when(jnp.logical_not(has_source))
            def _():
                outbox[d, b] = forcing(b).astype(jnp.bfloat16)

            @pl.when(has_target)
            def _():
                wave_copy(d, b, target).start()

            @pl.when(has_source)
            def _():
                side_copy(d, b, source).start()

            return carry

        return lax.fori_loop(0, batches, batch, carry)

    lax.fori_loop(0, 2, phase, 0)

    for b in range(batches):
        at = batch_rows(b)
        both = outbox[0, b].astype(jnp.float32) + outbox[1, b].astype(jnp.float32)
        traces_ref[0, at, :] = (both - forcing(b)).astype(jnp.bfloat16)

    def side(p, carry):
        e = (first + p) % 2
        source, target, has_source, has_target = neighbours(e)
        sign = 1 - 2 * e

        def batch(b, carry):
            at = batch_rows(b)

            @pl.when(has_target)
            def _():
                side_copy(e, b, source).wait_recv()
                moved = jnp.dot(sidebox[e, b], maps[1 - e], preferred_element_type=jnp.float32)
                total = acc[at, :] + jnp.where((depth_ref[at, :] - me) * sign <= 0, moved, 0.0)
                acc[at, :] = total
                residual_ref[0, at, :] = total.astype(jnp.bfloat16)

            return carry

        return lax.fori_loop(0, batches, batch, carry)

    lax.fori_loop(0, 2, side, 0)

    for d in range(2):
        source, target, has_source, has_target = neighbours(d)
        for b in range(batches):

            @pl.when(has_target)
            def _():
                wave_copy(d, b, target).wait_send()

            @pl.when(has_source)
            def _():
                side_copy(d, b, source).wait_send()


def shards(down_maps, up_maps, local_traces, src_depth, *, batches=BATCHES):
    source_rows, width = local_traces.shape
    n = lax.axis_size("layer")
    rows = source_rows // batches
    out = jax.ShapeDtypeStruct((1, source_rows, width), jnp.bfloat16)
    vmem = pl.BlockSpec(memory_space=pltpu.VMEM)
    anywhere = pl.BlockSpec(memory_space=pl.ANY)
    box = pltpu.VMEM((2, batches, rows, width), jnp.bfloat16)
    return pl.pallas_call(
        functools.partial(kernel, n, batches),
        out_shape=(out, out),
        in_specs=[anywhere, anywhere, vmem, vmem],
        out_specs=(vmem, vmem),
        scratch_shapes=[
            pltpu.VMEM((2, width, width), jnp.bfloat16),
            box,
            box,
            box,
            pltpu.VMEM((source_rows, width), jnp.float32),
            pltpu.SemaphoreType.DMA((2,)),
        ]
        + [pltpu.SemaphoreType.DMA((2, batches))] * 4,
        compiler_params=pltpu.CompilerParams(collective_id=0, has_side_effects=True),
        name="sweeps",
    )(down_maps, up_maps, local_traces, src_depth[:, None])


def solution(mesh):
    return jax.shard_map(
        shards,
        mesh=mesh,
        in_specs=(P("layer", None, None), P("layer", None, None), P("src", None), P("src")),
        out_specs=(P("layer", "src", None), P("layer", "src", None)),
        check_vma=False,
    )
```

time: 224 us -> 63.1 us (0.28)
  waiting for transfers between devices: 115 us -> 0 us
  starting transfers between devices: 84.9 us -> 0 us
  Pallas kernels: 0 us -> 57.6 us
  matrix products: 12.7 us -> 0 us
  other arithmetic: 5.94 us -> 0 us
  local copies, waits for them, and re-layouts: 1.46 us -> 4.62 us
    ppermute x34 -> x0, waiting for transfers between devices: 115 us -> none  [the longest x32 113 us: shifted(): return lax.ppermute(shard, axis, pairs)]
    ppermute x34 -> x0, starting transfers between devices: 84.9 us -> none  [the longest x32 79.1 us: shifted(): return lax.ppermute(shard, axis, pairs)]
    pallas_call x0 -> x1, Pallas kernels: none -> 57.6 us  [shards(): pl.pallas_call(functools.partial(kernel, n, batches), out_shape=(out, out...]
    dot_general x4 -> x0, matrix products: 12.7 us -> none  [the longest x2 7.29 us: apply_stack(): jnp.dot(current, maps[position], preferred_element_type=jnp.float32)]
    select_n x17 -> x0, other arithmetic: 5.16 us -> none  [the longest x16 4.13 us: advance(): jnp.where(active, new_block, previous)]
    unnamed x6 -> x2, local copies, waits for them, and re-layouts: 0.02 us -> 3.26 us
  transfers between devices with their start and end apart: 34 -> 0, of which waited for: 21 -> 0; matrix products, arithmetic and copies ran while one was open for 5% -> 0% of each run, Pallas kernels for 0% -> 0%
where the time goes in v1:
time: 63.1 us; the launch traced here: 62.9 us
  Pallas kernels  57.6 us (91%)
  local copies, waits for them, and re-layouts  4.62 us (7%)
  between operations  0.64 us (1%)
    pallas_call x1, Pallas kernels, shards(): pl.pallas_call(functools.partial(kernel, n, batches), out_shape=(out, out...  57.6 us
    unnamed x2, local copies, waits for them, and re-layouts  3.26 us
    broadcast_in_dim x1, local copies, waits for them, and re-layouts, shards(): src_depth[:, None]  1.36 us

profile of v1, /device:TPU:1, one launch (start us, length us, event | category | flops | bytes accessed | tf_op | source)
XLA Modules:
  0.0 62.9 jit_solution(15325309086574765596)
XLA Ops:
  0.6 1.4 %copy.6.depth_ref = s32[64,1]{1,0:T(8,128)} copy(s32[64,1]{0,1:T(1,128)} %bitcast.1) | data formatting | bytes 512 | tf_op jit(solution)/shard_map/broadcast_in_dim | solution.py:174
  2.0 57.6 %sweeps.1 = (bf16[1,64,1664]{2,1,0:T(8,128)(2,1)}, bf16[1,64,1664]{2,1,0:T(8,128)(2,1)}) custom-call(bf16[1,1664,1664]{2,1,0:T(8,128)(2,1)} %down_ref.1, bf16[1,1664,1664]{2,1,0:T(8,128)(2,1)} %up_ref.1, bf16[64,1664]{1,0:T(8,128)(2,1)} %local_ref.1, s32[64,1]{1,0:T(8,128)} %copy.6.depth_ref), custom_call_target="tpu_custom_call" | custom-call | tf_op jit(solution)/shard_map/sweeps/pallas_call | solution.py:158
  59.6 1.6 %copy.9 = bf16[1,64,1664]{2,1,0:T(8,128)(2,1)} copy(bf16[1,64,1664]{2,1,0:T(8,128)(2,1)} %get-tuple-element.4) | data formatting | bytes 425984
  61.3 1.6 %copy.10 = bf16[1,64,1664]{2,1,0:T(8,128)(2,1)} copy(bf16[1,64,1664]{2,1,0:T(8,128)(2,1)} %get-tuple-element.5) | data formatting | bytes 425984

commit v2 on v1

--- a/solution.py
+++ b/solution.py
@@ -9,11 +9,12 @@
 
 MESH = pl.DeviceIdType.MESH
 BATCHES = 4
+GRANT = 51 * 2**20
 
 
 def kernel(
     n, batches, down_ref, up_ref, local_ref, depth_ref, traces_ref, residual_ref,
-    maps, inbox, outbox, sidebox, acc, load_sem, wave_send, wave_recv, side_send, side_recv,
+    column, maps, inbox, outbox, sidebox, acc, load_sem, wave_send, wave_recv, side_send, side_recv,
 ):
     me = lax.axis_index("layer")
     rows = inbox.shape[2]
@@ -26,15 +27,13 @@
             (down_ref, up_ref)[d].at[0], maps.at[d], load_sem.at[d]
         )
 
-    @pl.when(first == 0)
-    def _():
-        load(0).start()
-        load(1).start()
+    for p in range(2):
+        for d in range(2):
+            needed = has_prev if d == 0 else has_next
 
-    @pl.when(first == 1)
-    def _():
-        load(1).start()
-        load(0).start()
+            @pl.when(jnp.logical_and((first + p) % 2 == d, needed))
+            def _():
+                load(d).start()
 
     acc[...] = jnp.zeros_like(acc)
     barrier = pltpu.get_barrier_semaphore()
@@ -49,11 +48,17 @@
 
     pl.semaphore_wait(barrier, has_prev.astype(jnp.int32) + has_next.astype(jnp.int32))
 
+    total_rows = depth_ref.shape[1]
+    square = (total_rows, total_rows)
+    spread = jnp.broadcast_to(depth_ref[...].astype(jnp.float32), square)
+    diagonal = lax.broadcasted_iota(jnp.int32, square, 0) == lax.broadcasted_iota(jnp.int32, square, 1)
+    column[...] = jnp.sum(jnp.where(diagonal, spread, 0.0), axis=1, keepdims=True)
+
     def batch_rows(b):
         return pl.ds(pl.multiple_of(b * rows, rows), rows)
 
     def forcing(b):
-        where = depth_ref[batch_rows(b), :] == me
+        where = column[batch_rows(b), :] == me.astype(jnp.float32)
         return jnp.where(where, local_ref[batch_rows(b), :].astype(jnp.float32), 0.0)
 
     def wave_copy(d, b, to):
@@ -80,7 +85,10 @@
     def phase(p, carry):
         d = (first + p) % 2
         source, target, has_source, has_target = neighbours(d)
-        pltpu.make_async_copy(down_ref.at[0], maps.at[d], load_sem.at[d]).wait()
+
+        @pl.when(has_source)
+        def _():
+            pltpu.make_async_copy(down_ref.at[0], maps.at[d], load_sem.at[d]).wait()
 
         def batch(b, carry):
             @pl.when(has_source)
@@ -97,13 +105,16 @@
             def _():
                 wave_copy(d, b, target).start()
 
-            @pl.when(has_source)
-            def _():
+            return carry
+
+        lax.fori_loop(0, batches, batch, carry)
+
+        @pl.when(has_source)
+        def _():
+            for b in range(batches):
                 side_copy(d, b, source).start()
 
-            return carry
-
-        return lax.fori_loop(0, batches, batch, carry)
+        return carry
 
     lax.fori_loop(0, 2, phase, 0)
 
@@ -124,7 +135,7 @@
             def _():
                 side_copy(e, b, source).wait_recv()
                 moved = jnp.dot(sidebox[e, b], maps[1 - e], preferred_element_type=jnp.float32)
-                total = acc[at, :] + jnp.where((depth_ref[at, :] - me) * sign <= 0, moved, 0.0)
+                total = acc[at, :] + jnp.where((column[at, :] - me.astype(jnp.float32)) * sign.astype(jnp.float32) <= 0.0, moved, 0.0)
                 acc[at, :] = total
                 residual_ref[0, at, :] = total.astype(jnp.bfloat16)
 
@@ -153,7 +164,7 @@
     rows = source_rows // batches
     out = jax.ShapeDtypeStruct((1, source_rows, width), jnp.bfloat16)
     vmem = pl.BlockSpec(memory_space=pltpu.VMEM)
-    anywhere = pl.BlockSpec(memory_space=pl.ANY)
+    anywhere = pl.BlockSpec(memory_space=pltpu.HBM)
     box = pltpu.VMEM((2, batches, rows, width), jnp.bfloat16)
     return pl.pallas_call(
         functools.partial(kernel, n, batches),
@@ -161,6 +172,7 @@
         in_specs=[anywhere, anywhere, vmem, vmem],
         out_specs=(vmem, vmem),
         scratch_shapes=[
+            pltpu.VMEM((source_rows, 1), jnp.float32),
             pltpu.VMEM((2, width, width), jnp.bfloat16),
             box,
             box,
@@ -169,9 +181,9 @@
             pltpu.SemaphoreType.DMA((2,)),
         ]
         + [pltpu.SemaphoreType.DMA((2, batches))] * 4,
-        compiler_params=pltpu.CompilerParams(collective_id=0, has_side_effects=True),
+        compiler_params=pltpu.CompilerParams(collective_id=0, has_side_effects=True, vmem_limit_bytes=GRANT),
         name="sweeps",
-    )(down_maps, up_maps, local_traces, src_depth[:, None])
+    )(down_maps, up_maps, local_traces, src_depth[None, :])
 
 
 def solution(mesh):

time: 63.1 us -> 59.1 us (0.937)
  Pallas kernels: 57.6 us -> 55.3 us
  local copies, waits for them, and re-layouts: 4.62 us -> 2.95 us
    pallas_call x1, Pallas kernels: 57.6 us -> 55.3 us  [shards(): pl.pallas_call(functools.partial(kernel, n, batches), out_shape=(out, out...]
    broadcast_in_dim x1 -> x0, local copies, waits for them, and re-layouts: 1.36 us -> none  [shards(): src_depth[:, None]]
    unnamed x2 -> x6, local copies, waits for them, and re-layouts: 3.26 us -> 2.95 us
where the time goes in v2:
time: 59.1 us; the launch traced here: 58.9 us
  Pallas kernels  55.3 us (94%)
  local copies, waits for them, and re-layouts  2.95 us (5%)
  between operations  0.65 us (1%)
    pallas_call x1, Pallas kernels, shards(): pl.pallas_call(functools.partial(kernel, n, batches), out_shape=(out, out...  55.3 us
    unnamed x6, local copies, waits for them, and re-layouts  2.95 us

profile of v2, /device:TPU:1, one launch (start us, length us, event | category | flops | bytes accessed | tf_op | source)
XLA Modules:
  0.0 58.9 jit_solution(15983751329044056987)
XLA Ops:
  0.6 0.0 copy-start
  0.6 0.9 %copy-done = bf16[64,1664]{1,0:T(8,128)(2,1)S(1)} copy-done((bf16[64,1664]{1,0:T(8,128)(2,1)S(1)}, bf16[64,1664]{1,0:T(8,128)(2,1)}, u32[]{:S(2)}) %copy-start) | copy-done | bytes 213016
  1.6 0.0 copy-start.1
  1.6 0.7 %copy-done.1 = s32[64]{0:T(128)S(1)} copy-done((s32[64]{0:T(128)S(1)}, s32[64]{0:T(128)}, u32[]{:S(2)}) %copy-start.1) | copy-done | bytes 280
  2.2 55.3 %sweeps.1 = (bf16[1,64,1664]{2,1,0:T(8,128)(2,1)S(1)}, bf16[1,64,1664]{2,1,0:T(8,128)(2,1)S(1)}) custom-call(bf16[1,1664,1664]{2,1,0:T(8,128)(2,1)} %down_ref.1, bf16[1,1664,1664]{2,1,0:T(8,128)(2,1)} %up_ref.1, bf16[64,1664]{1,0:T(8,128)(2,1)S(1)} %copy-done, s32[1,64]{1,0:T(1,128)S(1)} %bitcast.1), custom_call_target="tpu_custom_call" | custom-call | tf_op jit(solution)/shard_map/sweeps/pallas_call | solution.py:169
  57.5 0.7 %copy.8 = bf16[1,64,1664]{2,1,0:T(8,128)(2,1)} copy(bf16[1,64,1664]{2,1,0:T(8,128)(2,1)S(1)} %get-tuple-element.4) | data formatting | bytes 425984
  58.2 0.7 %copy.9 = bf16[1,64,1664]{2,1,0:T(8,128)(2,1)} copy(bf16[1,64,1664]{2,1,0:T(8,128)(2,1)S(1)} %get-tuple-element.5) | data formatting | bytes 425984
Async XLA Ops:
  0.6 0.9 %copy-start = (bf16[64,1664]{1,0:T(8,128)(2,1)S(1)}, bf16[64,1664]{1,0:T(8,128)(2,1)}, u32[]{:S(2)}) copy-start(bf16[64,1664]{1,0:T(8,128)(2,1)} %local_ref.1) | copy-start | bytes 638980
  1.6 0.7 %copy-start.1 = (s32[64]{0:T(128)S(1)}, s32[64]{0:T(128)}, u32[]{:S(2)}) copy-start(s32[64]{0:T(128)} %param.7) | copy-start | bytes 772
